TPU v7x, 32 devices: a whole 2x2x4 slice. The times are simulated.
32 devices in a mesh: emit: 4 (over z), elem: 8 (over y, x, core).
Axes of the slice: x: 2, y: 2, z: 4, core: 2. Of those that a mesh axis runs over, the one named last changes fastest.
Arguments:
- traces: float32 [256, 1024, 1024], P('emit', 'elem'), may hold values from -6 to 6
- codes: float32 [4, 2, 128], replicated, may hold values from -0.5 to 0.5
- code_of: int32 [256], replicated, may hold values from 0 to 3
- order: int32 [256], replicated, may hold values from 0 to 255, each once
- steer: float32 [256, 1024, 256], P(None, 'elem'), may hold values from -0.1875 to 0.1875
Outputs:
- beams: float32 [256, 256, 256], P('elem', 'emit')
Inputs may be any that keep to these rules, and one draw needn't show every extreme that they name: `order`: each value 0 to 255 appears exactly once.
All inputs are finite; a program needn't handle non-finite values.
Results may differ from a plain program's by a relative error of at most 0.000071.
Values sent between devices are 32-bit elements; how exact they have to be, the bound alone decides.
No kernel may reach another device: no remote copies, remote signals or barrier semaphores. Data moves between devices by JAX's collectives and lax.ppermute only.
A program may use at most 320 MiB of HBM per device.

v0:
```python
import jax
import jax.numpy as jnp
from jax import lax
from jax.sharding import PartitionSpec as P


def toeplitz_table(codes):
    taps = codes.shape[2]
    rows = jnp.arange(2 * taps, dtype=jnp.int32)[:, None]
    cols = jnp.arange(taps, dtype=jnp.int32)[None, :]
    offset = rows - cols
    inside = (offset >= 0) & (offset < taps)
    clipped = jnp.clip(offset, 0, taps - 1)
    in_phase = jnp.where(inside[None], codes[:, 0, :][:, clipped], 0.0)
    quadrature = jnp.where(inside[None], codes[:, 1, :][:, clipped], 0.0)
    return jnp.concatenate([in_phase, quadrature], axis=2)


def hadamard_signs(order, columns, emissions):
    parity = jnp.zeros((order.shape[0], columns.shape[0]), jnp.int32)
    for bit in range(emissions.bit_length()):
        parity = parity + (order[:, None] >> bit & columns[None, :] >> bit & 1)
    signs = (1 - 2 * (parity % 2)).astype(jnp.float32)
    return signs / jnp.sqrt(jnp.float32(emissions))


def spectral_table(samples, taps, bins):
    rows = jnp.arange(samples // taps * 2 * taps, dtype=jnp.int32)
    block = rows // (2 * taps)
    quad = rows // taps % 2
    sample = block * taps + rows % taps
    freqs = jnp.arange(bins, dtype=jnp.int32) - bins // 2
    phase = jnp.mod(sample[:, None] * freqs[None, :], samples).astype(jnp.float32)
    angle = phase * (2.0 * jnp.pi / samples)
    cosine = jnp.cos(angle)
    sine = jnp.sin(angle)
    is_quad = quad[:, None] == 1
    real_cols = jnp.where(is_quad, sine, cosine)
    imag_cols = jnp.where(is_quad, cosine, -sine)
    return jnp.concatenate([real_cols, imag_cols], axis=1) / jnp.sqrt(jnp.float32(samples))


def steer_bins(source, steer, count, contract):
    bins = steer.shape[0]
    half = steer.shape[2] // 2
    real_part = lax.slice_in_dim(source, 0, count, axis=0)
    imag_part = lax.dynamic_slice_in_dim(source, bins, count, 0)
    numbers = (((contract,), (1,)), ((0,), (0,)))
    first = lax.dot_general(real_part, steer, numbers, precision=lax.Precision.HIGHEST)
    second = lax.dot_general(imag_part, steer, numbers, precision=lax.Precision.HIGHEST)
    return jnp.concatenate(
        [first[..., :half] - second[..., half:], first[..., half:] + second[..., :half]], axis=2
    )


def per_device(traces, codes, code_of, order, steer):
    edev, mdev, samples = traces.shape
    ncode, taps = (codes.shape[0], codes.shape[2])
    emissions = order.shape[0]
    bins = steer.shape[0]
    bins_dev = bins // lax.axis_size("elem")
    nblock = samples // taps
    first = lax.axis_index("emit") * edev
    own_codes = lax.dynamic_slice_in_dim(code_of, first, edev)
    onehot = (own_codes[:, None] == jnp.arange(ncode, dtype=jnp.int32)[None, :]).astype(jnp.float32)
    table = toeplitz_table(codes)
    picked = jnp.einsum("ec,cjd->ejd", onehot, table, precision=lax.Precision.HIGHEST)
    blocks = traces.reshape(edev, mdev, nblock, taps)
    current = jnp.einsum(
        "emnj,ejd->emnd", blocks, picked[:, :taps, :], precision=lax.Precision.HIGHEST
    )
    following = jnp.einsum(
        "emnj,ejd->emnd", blocks, picked[:, taps:, :], precision=lax.Precision.HIGHEST
    )
    following = jnp.concatenate(
        [following[:, :, 1:], jnp.zeros((edev, mdev, 1, 2 * taps), jnp.float32)], axis=2
    )
    corr = (current + following).reshape(edev, mdev, nblock * 2 * taps)
    transform = spectral_table(samples, taps, bins)
    spectra = lax.dot_general(
        transform, corr, (((0,), (2,)), ((), ())), precision=lax.Precision.HIGHEST
    )
    columns = first + jnp.arange(edev, dtype=jnp.int32)
    hadamard = hadamard_signs(order, columns, emissions)
    coded = lax.psum_scatter(
        steer_bins(spectra, steer, bins_dev * lax.axis_size("elem"), 2),
        "elem",
        scatter_dimension=0,
        tiled=True,
    )
    folded = lax.dot_general(
        lax.all_gather(coded, "emit", axis=1, tiled=True),
        hadamard,
        (((1,), (0,)), ((), ())),
        precision=lax.Precision.HIGHEST,
    )
    beams = jnp.transpose(folded, (0, 2, 1))
    return beams


def solution(mesh):
    placed = (P("emit", "elem", None), P(), P(), P(), P(None, "elem", None))
    return jax.shard_map(
        per_device, mesh=mesh, in_specs=placed, out_specs=P("elem", "emit", None), check_vma=False
    )
```

profile of v0, /device:TPU:0, one launch (start us, length us, event | category | flops | bytes accessed | tf_op | source)
XLA Modules:
  0.0 971.7 jit_solution(796748638702718246)
XLA Ops:
  6.7 0.8 fusion.103
  7.5 0.1 copy.39
  7.6 109.0 %gather_fusion = f32[32768,4]{1,0:T(8,128)} fusion(f32[4,128]{0,1:T(8,128)S(1)} %bitcast.66, s32[32768]{0:T(1024)S(1)} %fusion.34), kind=kCustom, calls=%fused_computation | custom fusion | bytes 1179648 | tf_op jit(solution)/shard_map/gather | solution.py:14
  116.5 9.4 copy.17
  126.0 0.1 copy.40
  126.1 109.0 %gather_fusion.1 = f32[32768,4]{1,0:T(8,128)} fusion(f32[4,128]{0,1:T(8,128)S(1)} %bitcast.65, s32[32768]{0:T(1024)S(1)} %fusion.34), kind=kCustom, calls=%fused_computation.1 | custom fusion | bytes 1179648 | tf_op jit(solution)/shard_map/gather | solution.py:15
  235.0 9.4 copy.20
  244.6 0.3 select_bitcast_fusion.1
  244.9 7.0 fusion.26
  251.9 6.4 slice_bitcast_fusion.1
  258.3 65.5 %fusion.8 = f32[64,128,8,256]{1,3,2,0:T(8,128)} fusion(f32[64,128,256,1]{2,0,1,3:T(8,128)} %get-tuple-element.10, f32[64,128,1024]{2,1,0:T(8,128)} %param.5), kind=kOutput, calls=%fused_computation.9 | convolution fusion | flops 25769803776 | bytes 109051904 | tf_op jit(solution)/shard_map/emnj,ejd->emnd/dot_general | solution.py:72
  323.8 38.4 %slice.46 = f32[64,128,7,256]{1,3,2,0:T(8,128)} slice(f32[64,128,8,256]{1,3,2,0:T(8,128)} %fusion.8), slice={[0:64], [0:128], [1:8], [0:256]} | slice | bytes 117440512 | tf_op jit(solution)/shard_map/slice | solution.py:76
  362.2 88.9 %bitcast_add_fusion = f32[64,128,8,256]{1,3,2,0:T(8,128)} fusion(f32[64,128,7,256]{1,3,2,0:T(8,128)} %slice.46, f32[64,128,256,1]{2,0,1,3:T(8,128)} %get-tuple-element.9, f32[64,128,1024]{2,1,0:T(8,128)} %param.5), kind=kOutput, calls=%fused_computation.2 | convolution fusion | flops 25786580992 | bytes 167772160 | tf_op jit(solution)/shard_map/emnj,ejd->emnd/dot_general | solution.py:69
  451.1 8.4 fusion.32
  459.5 113.8 %fusion.18 = f32[512,64,128]{2,0,1:T(8,128)} fusion(f32[64,128,2048]{1,2,0:T(8,128)} %bitcast.13, f32[2048,256]{0,1:T(8,128)S(1)} %get-tuple-element.14, f32[2048,256]{0,1:T(8,128)S(1)} %get-tuple-element.13), kind=kOutput, calls=%fused_computation.23 | convolution fusion | flops 103081312256 | bytes 88080384 | tf_op jit(solution)/shard_map/dot_general | solution.py:80
  573.3 11.1 %fusion.102 = (f32[256,64,128]{2,0,1:T(8,128)}, f32[256,64,128]{2,0,1:T(8,128)}) fusion(f32[512,64,128]{2,0,1:T(8,128)} %fusion.18), kind=kLoop, calls=%fused_computation.140 | loop fusion | bytes 33554432 | tf_op jit(solution)/shard_map/slice | solution.py:46
  584.4 34.5 %fusion.13 = f32[256,64,256]{2,1,0:T(8,128)} fusion(f32[256,128,256]{2,1,0:T(8,128)} %param.9, f32[256,64,128]{2,0,1:T(8,128)} %get-tuple-element.8), kind=kOutput, calls=%fused_computation.17 | convolution fusion | flops 6442450944 | bytes 58720256 | tf_op jit(solution)/shard_map/dot_general | solution.py:50
  618.9 34.9 %fusion.15 = f32[256,64,256]{2,1,0:T(8,128)} fusion(f32[256,128,256]{2,1,0:T(8,128)} %param.9, f32[256,64,128]{2,0,1:T(8,128)} %get-tuple-element.7), kind=kOutput, calls=%fused_computation.19 | convolution fusion | flops 6442450944 | bytes 58720256 | tf_op jit(solution)/shard_map/dot_general | solution.py:49
  653.9 18.7 %slice_subtract_fusion = (f32[256,64,128]{2,1,0:T(8,128)}, f32[256,64,128]{2,1,0:T(8,128)}) fusion(f32[256,64,256]{2,1,0:T(8,128)} %fusion.13, f32[256,64,256]{2,1,0:T(8,128)} %fusion.15), kind=kLoop, calls=%fused_computation.12 | loop fusion | flops 4194304 | bytes 50331648 | tf_op jit(solution)/shard_map/sub | solution.py:52
  672.6 11.5 %pad_maximum_fusion = f32[256,64,256]{2,1,0:T(8,128)} fusion(f32[256,64,128]{2,1,0:T(8,128)} %get-tuple-element.6, f32[256,64,128]{2,1,0:T(8,128)} %get-tuple-element.5), kind=kLoop, calls=%fused_computation.10 | loop fusion | flops 4194304 | bytes 33554432 | tf_op jit(solution)/shard_map/concatenate | solution.py:51
  684.1 0.2 all-gather.2.cloned.1.call-start
  684.3 118.8 %reduce-scatter.2.cloned.1.call-done = f32[32,64,256]{2,1,0:T(8,128)} async-done(((f32[256,64,256]{2,1,0:T(8,128)}), f32[32,64,256]{2,1,0:T(8,128)}) %reduce-scatter.2.cloned.1.call-update) | async-done | bytes 2097168 | tf_op jit(solution)/shard_map/reduce_scatter | solution.py:85
  803.3 151.1 %all-gather.2.cloned.1.call-done = f32[32,256,256]{2,1,0:T(8,128)} async-done(((f32[32,64,256]{2,1,0:T(8,128)}), f32[32,256,256]{2,1,0:T(8,128)}) %all-gather.2.cloned.1.call-update) | async-done | bytes 8388624 | tf_op jit(solution)/shard_map/all_gather | solution.py:92
  954.4 10.3 %convolution_bitcast_fusion = f32[32,64,256]{2,1,0:T(8,128)} fusion(f32[32,256,256]{2,1,0:T(8,128)} %all-gather.2.cloned.1.call-done, s32[64]{0:T(128)S(1)} %get-tuple-element.26, s32[256]{0:T(256)S(1)} %get-tuple-element.24, s32[64]{0:T(128)S(1)} %get-tuple-element.27, s32[256]{0:T(256)S(1)} %get-tuple-element.25, s32[64]{0:T(128)S(1)} %get-tuple-element.28, ...), kind=kOutput, calls=%fused_computation.36 | convolution fusion | flops 1611284480 | bytes 10497280 | tf_op jit(solution)/shard_map/dot_general | solution.py:91
  (19 shorter events, 0.3 us)
Async XLA Ops:
  6.5 796.6 %reduce-scatter.2.cloned.1.call-start = ((), (), s32[]{:S(2)}) async-start(), calls=%async_computation.1 | async-start | bytes 18874368 | tf_op jit(solution)/shard_map/reduce_scatter | solution.py:85
  235.0 9.4 copy-start.1
  684.1 119.2 %copy-start = (s32[256]{0:T(256)S(1)}, s32[256]{0:T(256)}, u32[]{:S(2)}) copy-start(s32[256]{0:T(256)} %param.8) | copy-start | bytes 3076
  684.1 270.3 %all-gather.2.cloned.1.call-start = ((), (), s32[]{:S(2)}) async-start(), calls=%async_computation.2 | async-start | bytes 10485760 | tf_op jit(solution)/shard_map/all_gather | solution.py:92
Sparse Core Ops, SparseCore 0:
  684.2 118.8 reduce-scatter.1
  804.7 149.6 all-gather.1
where the time goes:
time: 979 us; the launch traced here: 972 us
  matrix products  355 us (36%)
  local copies, waits for them, and re-layouts  294 us (30%)
  waiting for transfers between devices  270 us (28%)
  other arithmetic  39.1 us (4%)
  between operations  13.7 us (1%)
    all_gather x1, waiting for transfers between devices, per_device(): lax.all_gather(coded, 'emit', axis=1, tiled=True)  151 us
    reduce_scatter x1, waiting for transfers between devices, per_device(): lax.psum_scatter(steer_bins(spectra, steer, bins_dev * lax.axis_size('ele...  119 us
    gather x2, local copies, waits for them, and re-layouts, toeplitz_table(): quadrature = jnp.where(inside[None], codes[:, 1, :][:, clipped], 0.0)  118 us
    gather x2, local copies, waits for them, and re-layouts, toeplitz_table(): in_phase = jnp.where(inside[None], codes[:, 0, :][:, clipped], 0.0)  118 us
    dot_general x1, matrix products, per_device(): lax.dot_general(transform, corr, (((0,), (2,)), ((), ())), precision=lax....  114 us
    dot_general x1, matrix products, per_device(): jnp.einsum('emnj,ejd->emnd', blocks, picked[:, :taps, :], precision=lax.P...  88.9 us
    dot_general x1, matrix products, per_device(): jnp.einsum('emnj,ejd->emnd', blocks, picked[:, taps:, :], precision=lax.P...  65.5 us
    slice x1, local copies, waits for them, and re-layouts, per_device(): following[:, :, 1:]  38.4 us
  transfers between devices with their start and end apart: 2, of which 2 were waited for; matrix products, arithmetic and copies ran while one was open for 0% of the time, Pallas kernels for 0%

commit v1 on v0

--- a/solution.py
+++ b/solution.py
@@ -2,6 +2,14 @@
 import jax.numpy as jnp
 from jax import lax
 from jax.sharding import PartitionSpec as P
+
+
+def gather_by_exchange(value, axis, dim):
+    count = lax.axis_size(axis)
+    repeats = [count if d == dim else 1 for d in range(value.ndim)]
+    return lax.all_to_all(
+        jnp.tile(value, repeats), axis, split_axis=dim, concat_axis=dim, tiled=True
+    )
 
 
 def toeplitz_table(codes):
@@ -89,7 +97,7 @@
         tiled=True,
     )
     folded = lax.dot_general(
-        lax.all_gather(coded, "emit", axis=1, tiled=True),
+        gather_by_exchange(coded, "emit", 1),
         hadamard,
         (((1,), (0,)), ((), ())),
         precision=lax.Precision.HIGHEST,

time: 979 us -> 1030 us (1.052)
  waiting for transfers between devices: 270 us -> 302 us
    all_to_all x0 -> x1, waiting for transfers between devices: none -> 183 us  [gather_by_exchange(): lax.all_to_all(jnp.tile(value, repeats), axis, split_axis=dim, concat_axi...]
    all_gather x1 -> x0, waiting for transfers between devices: 151 us -> none  [per_device(): lax.all_gather(coded, 'emit', axis=1, tiled=True)]
where the time goes in v1:
time: 1030 us; the launch traced here: 1020 us
  matrix products  359 us (35%)
  waiting for transfers between devices  302 us (29%)
  local copies, waits for them, and re-layouts  300 us (29%)
  other arithmetic  39.2 us (4%)
  between operations  13.7 us (1%)
    all_to_all x1, waiting for transfers between devices, gather_by_exchange(): lax.all_to_all(jnp.tile(value, repeats), axis, split_axis=dim, concat_axi...  183 us
    reduce_scatter x1, waiting for transfers between devices, per_device(): lax.psum_scatter(steer_bins(spectra, steer, bins_dev * lax.axis_size('ele...  119 us
    gather x2, local copies, waits for them, and re-layouts, toeplitz_table(): quadrature = jnp.where(inside[None], codes[:, 1, :][:, clipped], 0.0)  118 us
    gather x2, local copies, waits for them, and re-layouts, toeplitz_table(): in_phase = jnp.where(inside[None], codes[:, 0, :][:, clipped], 0.0)  118 us
    dot_general x1, matrix products, per_device(): lax.dot_general(transform, corr, (((0,), (2,)), ((), ())), precision=lax....  114 us
    dot_general x1, matrix products, per_device(): jnp.einsum('emnj,ejd->emnd', blocks, picked[:, :taps, :], precision=lax.P...  88.7 us
    dot_general x1, matrix products, per_device(): jnp.einsum('emnj,ejd->emnd', blocks, picked[:, taps:, :], precision=lax.P...  65.5 us
    slice x1, local copies, waits for them, and re-layouts, per_device(): following[:, :, 1:]  38.4 us
  transfers between devices with their start and end apart: 2, of which 2 were waited for; matrix products, arithmetic and copies ran while one was open for 0% of the time, Pallas kernels for 0%

profile of v1, /device:TPU:0, one launch (start us, length us, event | category | flops | bytes accessed | tf_op | source)
XLA Modules:
  0.0 1019.4 jit_solution(5315561227958234504)
XLA Ops:
  6.7 0.8 fusion.108
  7.6 108.3 %gather_fusion = f32[32768,4]{1,0:T(8,128)} fusion(f32[4,128]{0,1:T(8,128)S(1)} %bitcast.66, s32[32768]{0:T(1024)S(1)} %fusion.39), kind=kCustom, calls=%fused_computation | custom fusion | bytes 1179648 | tf_op jit(solution)/shard_map/gather | solution.py:22
  115.9 9.4 copy.30
  125.4 108.3 %gather_fusion.1 = f32[32768,4]{1,0:T(8,128)} fusion(f32[4,128]{0,1:T(8,128)S(1)} %bitcast.65, s32[32768]{0:T(1024)S(1)} %fusion.39), kind=kCustom, calls=%fused_computation.1 | custom fusion | bytes 1179648 | tf_op jit(solution)/shard_map/gather | solution.py:23
  233.8 9.4 copy.33
  243.3 0.3 select_bitcast_fusion.1
  243.6 7.0 fusion.31
  250.6 6.4 slice_bitcast_fusion.1
  257.0 65.5 %fusion.8 = f32[64,128,8,256]{1,3,2,0:T(8,128)} fusion(f32[64,128,256,1]{2,0,1,3:T(8,128)} %get-tuple-element.10, f32[64,128,1024]{2,1,0:T(8,128)} %param.5), kind=kOutput, calls=%fused_computation.9 | convolution fusion | flops 25769803776 | bytes 109051904 | tf_op jit(solution)/shard_map/emnj,ejd->emnd/dot_general | solution.py:80
  322.5 38.4 %slice.46 = f32[64,128,7,256]{1,3,2,0:T(8,128)} slice(f32[64,128,8,256]{1,3,2,0:T(8,128)} %fusion.8), slice={[0:64], [0:128], [1:8], [0:256]} | slice | bytes 117440512 | tf_op jit(solution)/shard_map/slice | solution.py:84
  360.9 88.7 %bitcast_add_fusion = f32[64,128,8,256]{1,3,2,0:T(8,128)} fusion(f32[64,128,7,256]{1,3,2,0:T(8,128)} %slice.46, f32[64,128,256,1]{2,0,1,3:T(8,128)} %get-tuple-element.9, f32[64,128,1024]{2,1,0:T(8,128)} %param.5), kind=kOutput, calls=%fused_computation.2 | convolution fusion | flops 25786580992 | bytes 167772160 | tf_op jit(solution)/shard_map/emnj,ejd->emnd/dot_general | solution.py:77
  449.6 8.4 fusion.37
  458.1 113.8 %fusion.20 = f32[512,64,128]{2,0,1:T(8,128)} fusion(f32[64,128,2048]{1,2,0:T(8,128)} %bitcast.13, f32[2048,256]{0,1:T(8,128)S(1)} %get-tuple-element.14, f32[2048,256]{0,1:T(8,128)S(1)} %get-tuple-element.13), kind=kOutput, calls=%fused_computation.25 | convolution fusion | flops 103081312256 | bytes 88080384 | tf_op jit(solution)/shard_map/dot_general | solution.py:88
  571.9 11.1 %fusion.107 = (f32[256,64,128]{2,0,1:T(8,128)}, f32[256,64,128]{2,0,1:T(8,128)}) fusion(f32[512,64,128]{2,0,1:T(8,128)} %fusion.20), kind=kLoop, calls=%fused_computation.142 | loop fusion | bytes 33554432 | tf_op jit(solution)/shard_map/slice | solution.py:54
  582.9 34.5 %fusion.15 = f32[256,64,256]{2,1,0:T(8,128)} fusion(f32[256,128,256]{2,1,0:T(8,128)} %param.9, f32[256,64,128]{2,0,1:T(8,128)} %get-tuple-element.8), kind=kOutput, calls=%fused_computation.19 | convolution fusion | flops 6442450944 | bytes 58720256 | tf_op jit(solution)/shard_map/dot_general | solution.py:58
  617.5 34.9 %fusion.17 = f32[256,64,256]{2,1,0:T(8,128)} fusion(f32[256,128,256]{2,1,0:T(8,128)} %param.9, f32[256,64,128]{2,0,1:T(8,128)} %get-tuple-element.7), kind=kOutput, calls=%fused_computation.21 | convolution fusion | flops 6442450944 | bytes 58720256 | tf_op jit(solution)/shard_map/dot_general | solution.py:57
  652.4 18.7 %slice_subtract_fusion = (f32[256,64,128]{2,1,0:T(8,128)}, f32[256,64,128]{2,1,0:T(8,128)}) fusion(f32[256,64,256]{2,1,0:T(8,128)} %fusion.15, f32[256,64,256]{2,1,0:T(8,128)} %fusion.17), kind=kLoop, calls=%fused_computation.12 | loop fusion | flops 4194304 | bytes 50331648 | tf_op jit(solution)/shard_map/sub | solution.py:60
  671.0 11.7 %pad_maximum_fusion = f32[256,64,256]{2,1,0:T(8,128)} fusion(f32[256,64,128]{2,1,0:T(8,128)} %get-tuple-element.6, f32[256,64,128]{2,1,0:T(8,128)} %get-tuple-element.5), kind=kLoop, calls=%fused_computation.10 | loop fusion | flops 4194304 | bytes 33554432 | tf_op jit(solution)/shard_map/concatenate | solution.py:59
  682.7 119.1 %reduce-scatter.2.cloned.1.call-done = f32[32,64,256]{2,1,0:T(8,128)} async-done(((f32[256,64,256]{2,1,0:T(8,128)}), f32[32,64,256]{2,1,0:T(8,128)}) %reduce-scatter.2.cloned.1.call-update) | async-done | bytes 2097168 | tf_op jit(solution)/shard_map/reduce_scatter | solution.py:93
  801.8 2.8 copy.41
  804.6 4.3 tile.4
  808.9 5.8 all-to-all-start
  814.8 183.1 %all-to-all-done = f32[32,256,256]{2,0,1:T(8,128)} async-done(((f32[32,256,256]{2,0,1:T(8,128)}), f32[32,256,256]{2,0,1:T(8,128)}, u32[]{:S(2)}, u32[]{:S(2)}) %all-to-all-start) | async-done | bytes 8388640 | tf_op jit(solution)/shard_map/all_to_all | solution.py:10
  997.9 14.5 %fusion.28 = f32[32,64,256]{2,1,0:T(8,128)} fusion(f32[32,256,256]{2,0,1:T(8,128)} %all-to-all-done, s32[64]{0:T(128)S(1)} %get-tuple-element.26, s32[256]{0:T(256)S(1)} %get-tuple-element.24, s32[64]{0:T(128)S(1)} %get-tuple-element.27, s32[256]{0:T(256)S(1)} %get-tuple-element.25, s32[64]{0:T(128)S(1)} %get-tuple-element.28, ...), kind=kOutput, calls=%fused_computation.38 | convolution fusion | flops 1611284480 | bytes 10497280 | tf_op jit(solution)/shard_map/dot_general | solution.py:99
  (20 shorter events, 0.5 us)
Async XLA Ops:
  6.5 795.3 %reduce-scatter.2.cloned.1.call-start = ((), (), s32[]{:S(2)}) async-start(), calls=%async_computation.2 | async-start | bytes 18874368 | tf_op jit(solution)/shard_map/reduce_scatter | solution.py:93
  233.8 9.4 copy-start.1
  808.9 5.8 copy-start
  808.9 189.0 %all-to-all-start = ((f32[32,256,256]{2,0,1:T(8,128)}), f32[32,256,256]{2,0,1:T(8,128)}, u32[]{:S(2)}, u32[]{:S(2)}) async-start(f32[32,256,256]{2,0,1:T(8,128)} %bitcast.67), calls=%async_computation.1 | async-start | bytes 16777216 | tf_op jit(solution)/shard_map/all_to_all | solution.py:10
Sparse Core Ops, SparseCore 0:
  682.9 118.9 reduce-scatter.1
